TPU v7x, 256 devices: a whole 4x4x8 slice. The times are simulated.
256 devices in a mesh: scen: 64 (over y, z, core), link: 4 (over x).
Axes of the slice: x: 4, y: 4, z: 8, core: 2. Of those that a mesh axis runs over, the one named last changes fastest.
Arguments:
- factor_inv: bfloat16 [128, 1024, 1024], P('scen'), may hold values from -0.1875 to 0.1875
- coupling: bfloat16 [128, 1024, 1024], P('scen', None, 'link'), may hold values from -0.375 to 0.375
- first_diag: float32 [128, 128], P('scen'), may hold values from 1 to 10
- pattern: int32 [128, 8], P('scen'), may hold values from 0 to 127, as said below
Outputs:
- panel: float32 [16384, 128], P('scen')
- trailing: float32 [16384, 16384], P('scen', 'link')
Inputs may be any that keep to these rules, and one draw needn't show every extreme that they name: `pattern`: slot t of a scenario names a block of column range t // 2, that is, a block p with p // 32 = t // 2. The 2 scenarios of rows s * 2 to (s + 1) * 2 - 1 name every block at most once among them, and at most 1 block of any one group of blocks with the same p // 2. The first scenario of every such set names block 0 in slot 0.
All inputs are finite; a program needn't handle non-finite values.
Results may differ from a plain program's by a relative error of at most 0.0005.
Values may be sent and summed in bfloat16 or wider, within the bound.
No kernel may reach another device: no remote copies, remote signals or barrier semaphores. Data moves between devices by JAX's collectives and lax.ppermute only.
A program may use at most 128 MiB of HBM per device.

v0:
```python
import jax
import jax.numpy as jnp
from jax import lax
from jax.sharding import PartitionSpec as P


def broadcast(value, axis, source):
    kept = jnp.where(lax.axis_index(axis) == source, value, 0).astype(value.dtype)
    return lax.psum(kept, axis)


def per_device(factor_inv, coupling, first_diag, pattern):
    tile_size = first_diag.shape[1]
    rows_own = first_diag.shape[0]
    scen_count = lax.axis_size("scen")
    link_count = lax.axis_size("link")
    scen_pos = lax.axis_index("scen")
    link_pos = lax.axis_index("link")
    block_count = rows_own * scen_count
    per_link = block_count // link_count
    col_width = coupling.shape[2]
    slot_count = col_width // tile_size
    own_slabs = jnp.einsum(
        "snm,smc->snc", factor_inv, coupling, preferred_element_type=jnp.float32
    ).astype(jnp.bfloat16)
    contrib = jnp.einsum(
        "snr,snc->src",
        lax.all_gather(own_slabs, "link", axis=2, tiled=True),
        own_slabs,
        preferred_element_type=jnp.float32,
    )
    scen_here = contrib.shape[0]
    spread = pattern.shape[1]
    blocks = pattern.reshape(-1)
    tile_rows = contrib.reshape(scen_here * spread, tile_size, col_width)
    own_cols = (
        lax.dynamic_slice_in_dim(pattern, link_pos * slot_count, slot_count, 1)
        - link_pos * per_link
    )
    col_rows = jnp.broadcast_to(own_cols[:, None, :], (scen_here, spread, slot_count)).reshape(
        scen_here * spread, slot_count
    )
    col_range = jnp.arange(per_link, dtype=jnp.int32)
    outgoing = jnp.zeros((block_count, tile_size, col_width), jnp.float32).at[blocks].set(tile_rows)
    labels = jnp.full((block_count, slot_count), -1, jnp.int32).at[blocks].set(col_rows)
    arrived, arrived_cols = (
        lax.all_to_all(outgoing, "scen", split_axis=0, concat_axis=0, tiled=True),
        lax.all_to_all(labels, "scen", split_axis=0, concat_axis=0, tiled=True),
    )
    selector = (arrived_cols[:, :, None] == col_range[None, None, :]).astype(jnp.float32)
    selector = selector.reshape(scen_count, rows_own, slot_count, per_link)
    arrived = arrived.reshape(scen_count, rows_own, tile_size, slot_count, tile_size)
    summed = jnp.einsum("srkc,srxky->rxcy", selector, arrived, precision=lax.Precision.HIGHEST)
    global_rows = scen_pos * rows_own + jnp.arange(rows_own, dtype=jnp.int32)
    global_cols = link_pos * per_link + col_range
    on_diagonal = (global_rows[:, None] == global_cols[None, :]).astype(jnp.float32)
    unit_matrix = jnp.eye(tile_size, dtype=jnp.float32)
    diag_part = (
        on_diagonal[:, None, :, None]
        * (first_diag[:, :, None] * unit_matrix[None, :, :])[:, :, None, :]
    )
    schur = (summed + diag_part).reshape(rows_own * tile_size, per_link * tile_size)
    corner = broadcast(schur[:tile_size, :tile_size], "scen", 0)
    lead_factor = jnp.linalg.cholesky(corner)
    solved = jax.scipy.linalg.solve_triangular(lead_factor, schur[:, :tile_size].T, lower=True).T
    top_block = jnp.where(scen_pos == 0, lead_factor, solved[:tile_size])
    panel_mine = broadcast(jnp.concatenate([top_block, solved[tile_size:]], axis=0), "link", 0)
    gathered = lax.all_gather(panel_mine, "scen", axis=0, tiled=True)
    partner = lax.dynamic_slice_in_dim(
        gathered, link_pos * per_link * tile_size, per_link * tile_size, 0
    )
    trailing = schur - jnp.dot(
        panel_mine, partner.T, precision=lax.Precision.HIGHEST, preferred_element_type=jnp.float32
    )
    return (panel_mine, trailing)


def solution(mesh):
    in_specs = (P("scen", None, None), P("scen", None, "link"), P("scen", None), P("scen", None))
    out_specs = (P("scen", None), P("scen", "link"))
    return jax.shard_map(
        per_device, mesh=mesh, in_specs=in_specs, out_specs=out_specs, check_vma=False
    )
```

profile of v0, /device:TPU:1, one launch (start us, length us, event | category | flops | bytes accessed | tf_op | source)
XLA Modules:
  0.0 855.0 jit_solution(7507519871486025331)
XLA Ops:
  7.2 0.0 copy-start
  7.2 0.0 all-gather.3.cloned.1.call-start
  7.2 1.2 copy-done
  8.4 4.4 convolution_convert_fusion
  12.8 0.0 all-gather.3.cloned.1.call-update
  12.8 0.1 reshape.110
  12.9 0.1 dynamic-slice_subtract_fusion
  13.0 0.7 scatter_custom_fusion.1
  13.7 1.1 copy.30
  14.8 13.1 %all-to-all-start.1 = ((s32[64,2,2]{1,2,0:T(2,128)}), s32[64,2,2]{1,2,0:T(2,128)S(1)}, u32[]{:S(2)}, u32[]{:S(2)}) async-start(s32[64,2,2]{1,2,0:T(2,128)} %copy.30), calls=%async_computation.1 | async-start | bytes 131072 | tf_op jit(solution)/shard_map/all_to_all | solution.py:48
  27.9 41.4 %all-gather.3.cloned.1.call-done = bf16[2,1024,1024]{2,1,0:T(8,128)(2,1)} async-done(((bf16[2,1024,256]{2,1,0:T(8,128)(2,1)}), bf16[2,1024,1024]{2,1,0:T(8,128)(2,1)}) %all-gather.3.cloned.1.call-update) | async-done | bytes 4194320 | tf_op jit(solution)/shard_map/all_gather | solution.py:28
  69.3 4.2 fusion.15
  73.5 7.8 broadcast_in_dim.13
  81.4 3.7 scatter_fusion
  85.1 0.0 all-to-all-done.1
  85.1 12.4 %all-to-all-start = ((f32[128,128,256]{2,1,0:T(8,128)}), f32[128,128,256]{2,1,0:T(8,128)}, u32[]{:S(2)}, u32[]{:S(2)}) async-start(f32[128,128,256]{2,1,0:T(8,128)} %scatter_fusion), calls=%async_computation | async-start | bytes 33554432 | tf_op jit(solution)/shard_map/all_to_all | solution.py:47
  97.5 0.2 all-reduce.3.cloned.1.call-start
  97.8 0.1 compare_convert_fusion
  97.8 0.1 broadcast_multiply_fusion
  97.9 0.1 copy.31
  98.0 365.0 %all-to-all-done = f32[128,128,256]{2,1,0:T(8,128)} async-done(((f32[128,128,256]{2,1,0:T(8,128)}), f32[128,128,256]{2,1,0:T(8,128)}, u32[]{:S(2)}, u32[]{:S(2)}) %all-to-all-start) | async-done | bytes 16777248 | tf_op jit(solution)/shard_map/all_to_all | solution.py:47
  463.0 17.4 %copy.26 = f32[128,128,256]{1,2,0:T(8,128)} copy(f32[128,128,256]{2,1,0:T(8,128)} %all-to-all-done) | data formatting | bytes 33554432 | tf_op jit(solution)/shard_map/all_to_all | solution.py:47
  480.4 16.5 %copy.32 = f32[64,2,128,2,128]{4,0,3,2,1:T(8,128)} copy(f32[64,2,128,2,128]{2,4,3,1,0:T(8,128)} %bitcast.40) | data formatting | bytes 33554432 | tf_op jit(solution)/shard_map/reshape | solution.py:52
  496.9 9.5 %bitcast_add_fusion = f32[2,128,32,128]{3,2,1,0:T(8,128)S(1)} fusion(f32[64,2,128,2,128]{4,0,3,2,1:T(8,128)} %copy.32, f32[2,128,128]{2,1,0:T(8,128)S(1)} %broadcast_multiply_fusion, f32[2,32]{1,0:T(2,128)S(1)} %compare_convert_fusion, s32[64,2,2]{0,2,1:T(2,128)S(1)} %copy.31), kind=kOutput, calls=%fused_computation.4 | convolution fusion | flops 1612718080 | bytes 21103872 | tf_op jit(solution)/shard_map/srkc,srxky->rxcy/dot_general | solution.py:53
  506.5 3.9 copy.45
  510.4 0.0 copy-start.3
  510.4 2.0 copy-done.3
  512.4 0.6 slice_select_fusion.1
  513.0 0.0 all-reduce.3.cloned.1.call-update
  513.0 0.3 all-reduce.5.cloned.1.call-start
  513.3 167.0 %all-reduce.3.cloned.1.call-done = f32[128,128]{1,0:T(8,128)} async-done(((f32[128,128]{1,0:T(8,128)}), f32[128,128]{1,0:T(8,128)}) %all-reduce.3.cloned.1.call-update) | async-done | bytes 65552 | tf_op jit(solution)/shard_map/psum | solution.py:9
  680.3 0.9 copy.33
  681.2 0.9 fusion.4
  682.1 11.7 %cholesky.19 = f32[128,128]{1,0:T(8,128)S(1)} custom-call(f32[128,128]{1,0:T(8,128)S(1)} %fusion.4), custom_call_target="Cholesky" | custom-call | tf_op jit(solution)/shard_map/jit(cholesky)/cholesky | solution.py:64
  693.8 0.6 compare_reduce_fusion
  694.5 0.7 select_bitcast_fusion
  695.1 9.8 %custom-call.7 = f32[1,128,128]{1,2,0:T(8,128)S(1)} custom-call(f32[1,128,128]{2,1,0:T(8,128)S(1)} %select_bitcast_fusion), custom_call_target="InvertDiagBlocksLowerTriangular" | custom-call | tf_op jit(solution)/shard_map/jit(_solve_triangular)/triangular_solve | solution.py:65
  704.9 1.2 fusion.1
  706.1 0.7 slice_select_fusion
  706.8 0.7 maximum_select_fusion
  707.4 0.0 all-reduce.5.cloned.1.call-update
  707.5 0.3 all-gather.5.cloned.1.call-start
  707.8 41.0 %all-reduce.5.cloned.1.call-done = f32[256,128]{1,0:T(8,128)} async-done(((f32[256,128]{1,0:T(8,128)}), f32[256,128]{1,0:T(8,128)}) %all-reduce.5.cloned.1.call-update) | async-done | bytes 131088 | tf_op jit(solution)/shard_map/psum | solution.py:9
  748.7 0.0 all-gather.5.cloned.1.call-update
  748.8 0.0 copy-start.1
  748.8 88.6 %all-gather.5.cloned.1.call-done = f32[16384,128]{1,0:T(8,128)} async-done(((f32[256,128]{1,0:T(8,128)}), f32[16384,128]{1,0:T(8,128)}) %all-gather.5.cloned.1.call-update) | async-done | bytes 8388624 | tf_op jit(solution)/shard_map/all_gather | solution.py:68
  837.4 10.4 %convolution_subtract_fusion = f32[256,4096]{1,0:T(8,128)} fusion(f32[256,128]{1,0:T(8,128)} %all-reduce.5.cloned.1.call-done, f32[16384,128]{1,0:T(8,128)} %all-gather.5.cloned.1.call-done, s32[]{:T(128)S(6)} %select_n.51, f32[32,8,32,128]{3,2,1,0:T(8,128)} %bitcast.42), kind=kOutput, calls=%fused_computation.2 | convolution fusion | flops 1611661312 | bytes 10616836 | tf_op jit(solution)/shard_map/dot_general | solution.py:72
  847.8 0.7 copy.49
  (14 shorter events, 0.1 us)
Async XLA Ops:
  7.2 1.2 copy-start
  7.2 5.7 copy-start.6
  7.2 62.1 %all-gather.3.cloned.1.call-start = ((), (), s32[]{:S(2)}) async-start(), calls=%async_computation.2 | async-start | bytes 5242880 | tf_op jit(solution)/shard_map/all_gather | solution.py:28
  14.8 70.3 %all-to-all-start.1 = ((s32[64,2,2]{1,2,0:T(2,128)}), s32[64,2,2]{1,2,0:T(2,128)S(1)}, u32[]{:S(2)}, u32[]{:S(2)}) async-start(s32[64,2,2]{1,2,0:T(2,128)} %copy.30), calls=%async_computation.1 | async-start | bytes 131072 | tf_op jit(solution)/shard_map/all_to_all | solution.py:48
  85.1 12.8 %copy-start.5 = (f32[2,128]{1,0:T(2,128)S(1)}, f32[2,128]{1,0:T(2,128)}, u32[]{:S(2)}) copy-start(f32[2,128]{1,0:T(2,128)} %param.6) | copy-start | bytes 3076
  85.1 377.9 %all-to-all-start = ((f32[128,128,256]{2,1,0:T(8,128)}), f32[128,128,256]{2,1,0:T(8,128)}, u32[]{:S(2)}, u32[]{:S(2)}) async-start(f32[128,128,256]{2,1,0:T(8,128)} %scatter_fusion), calls=%async_computation | async-start | bytes 33554432 | tf_op jit(solution)/shard_map/all_to_all | solution.py:47
  97.5 582.8 %all-reduce.3.cloned.1.call-start = ((), (), s32[]{:S(2)}) async-start(), calls=%async_computation.3 | async-start | bytes 131072 | tf_op jit(solution)/shard_map/psum | solution.py:9
  506.4 3.9 copy-start.2
  510.4 2.0 copy-start.3
  513.0 235.7 %all-reduce.5.cloned.1.call-start = ((), (), s32[]{:S(2)}) async-start(), calls=%async_computation.4 | async-start | bytes 262144 | tf_op jit(solution)/shard_map/psum | solution.py:9
  707.5 129.9 %all-gather.5.cloned.1.call-start = ((), (), s32[]{:S(2)}) async-start(), calls=%async_computation.5 | async-start | bytes 8519680 | tf_op jit(solution)/shard_map/all_gather | solution.py:68
  748.8 99.7 %copy-start.1 = (bf16[2,1024,256]{2,1,0:T(8,128)(2,1)S(1)}, bf16[2,1024,256]{2,1,0:T(8,128)(2,1)}, u32[]{:S(2)}) copy-start(bf16[2,1024,256]{2,1,0:T(8,128)(2,1)} %param.5) | copy-start | bytes 3145732
  748.8 99.0 %copy-start.4 = (f32[256,128]{1,0:T(8,128)S(1)}, f32[256,128]{1,0:T(8,128)}, u32[]{:S(2)}) copy-start(f32[256,128]{1,0:T(8,128)} %all-reduce.5.cloned.1.call-done) | copy-start | bytes 393220
Sparse Core Ops, SparseCore 0:
  12.9 56.2 all-gather.2
  513.2 167.0 all-reduce.2
  707.6 41.0 all-reduce.4
  751.4 85.9 all-gather.4
where the time goes:
time: 856 us; the launch traced here: 855 us
  waiting for transfers between devices  703 us (82%)
  local copies, waits for them, and re-layouts  56.1 us (7%)
  matrix products  29.7 us (3%)
  starting transfers between devices  26.4 us (3%)
  other arithmetic  25.9 us (3%)
  between operations  14 us (2%)
    all_to_all x1, waiting for transfers between devices, per_device(): lax.all_to_all(outgoing, 'scen', split_axis=0, concat_axis=0, tiled=True)  365 us
    psum x2, waiting for transfers between devices, broadcast(): return lax.psum(kept, axis)  208 us
    all_gather x1, waiting for transfers between devices, per_device(): gathered = lax.all_gather(panel_mine, 'scen', axis=0, tiled=True)  88.6 us
    all_gather x1, waiting for transfers between devices, per_device(): lax.all_gather(own_slabs, 'link', axis=2, tiled=True)  41.4 us
    all_to_all x1, local copies, waits for them, and re-layouts, per_device(): lax.all_to_all(outgoing, 'scen', split_axis=0, concat_axis=0, tiled=True)  17.4 us
  transfers between devices with their start and end apart: 6, of which 5 were waited for; matrix products, arithmetic and copies ran while one was open for 2% of the time, Pallas kernels for 0%

commit v1 on v0

--- a/solution.py
+++ b/solution.py
@@ -6,7 +6,7 @@
 
 def broadcast(value, axis, source):
     kept = jnp.where(lax.axis_index(axis) == source, value, 0).astype(value.dtype)
-    return lax.psum(kept, axis)
+    return jnp.sum(lax.all_gather(kept, axis), axis=0)
 
 
 def per_device(factor_inv, coupling, first_diag, pattern):

time: 856 us -> 728 us (0.85)
  waiting for transfers between devices: 703 us -> 564 us
  blocking collectives: 0 us -> 11.3 us
    psum x2 -> x0, waiting for transfers between devices: 208 us -> none  [broadcast(): return lax.psum(kept, axis)]
    all_gather x0 -> x1, waiting for transfers between devices: none -> 75.6 us  [broadcast(): return jnp.sum(lax.all_gather(kept, axis), axis=0)]
    all_gather x0 -> x1, blocking collectives: none -> 11.3 us  [broadcast(): return jnp.sum(lax.all_gather(kept, axis), axis=0)]
  transfers between devices with their start and end apart: 6 -> 5, of which waited for: 5 -> 4; matrix products, arithmetic and copies ran while one was open for 2% -> 2% of each run, Pallas kernels for 0% -> 0%
where the time goes in v1:
time: 728 us; the launch traced here: 727 us
  waiting for transfers between devices  564 us (77%)
  local copies, waits for them, and re-layouts  54.6 us (8%)
  matrix products  29.7 us (4%)
  other arithmetic  27.5 us (4%)
  starting transfers between devices  26.1 us (4%)
  between operations  14 us (2%)
  blocking collectives  11.3 us (2%)
    all_to_all x1, waiting for transfers between devices, per_device(): lax.all_to_all(outgoing, 'scen', split_axis=0, concat_axis=0, tiled=True)  365 us
    all_gather x1, waiting for transfers between devices, per_device(): gathered = lax.all_gather(panel_mine, 'scen', axis=0, tiled=True)  82.2 us
    all_gather x1, waiting for transfers between devices, broadcast(): return jnp.sum(lax.all_gather(kept, axis), axis=0)  75.6 us
    all_gather x1, waiting for transfers between devices, per_device(): lax.all_gather(own_slabs, 'link', axis=2, tiled=True)  41.4 us
    all_to_all x1, local copies, waits for them, and re-layouts, per_device(): lax.all_to_all(outgoing, 'scen', split_axis=0, concat_axis=0, tiled=True)  17.4 us
    reshape x1, local copies, waits for them, and re-layouts, per_device(): arrived.reshape(scen_count, rows_own, tile_size, slot_count, tile_size)  16.5 us
  transfers between devices with their start and end apart: 5, of which 4 were waited for; matrix products, arithmetic and copies ran while one was open for 2% of the time, Pallas kernels for 0%

profile of v1, /device:TPU:1, one launch (start us, length us, event | category | flops | bytes accessed | tf_op | source)
XLA Modules:
  0.0 727.4 jit_solution(15170759094044756831)
XLA Ops:
  7.2 0.0 copy-start
  7.2 0.0 copy-start.5
  7.2 0.0 all-gather.5.cloned.1.call-start
  7.2 1.2 copy-done
  8.4 4.4 convolution_convert_fusion
  12.8 0.0 all-gather.5.cloned.1.call-update
  12.8 0.0 copy-done.5
  12.8 0.1 reshape.139
  12.9 0.1 dynamic-slice_subtract_fusion
  13.0 0.7 scatter_custom_fusion.1
  13.7 1.1 copy.30
  14.8 13.1 %all-to-all-start.1 = ((s32[64,2,2]{1,2,0:T(2,128)}), s32[64,2,2]{1,2,0:T(2,128)S(1)}, u32[]{:S(2)}, u32[]{:S(2)}) async-start(s32[64,2,2]{1,2,0:T(2,128)} %copy.30), calls=%async_computation.1 | async-start | bytes 131072 | tf_op jit(solution)/shard_map/all_to_all | solution.py:48
  27.9 41.4 %all-gather.5.cloned.1.call-done = bf16[2,1024,1024]{2,1,0:T(8,128)(2,1)} async-done(((bf16[2,1024,256]{2,1,0:T(8,128)(2,1)}), bf16[2,1024,1024]{2,1,0:T(8,128)(2,1)}) %all-gather.5.cloned.1.call-update) | async-done | bytes 4194320 | tf_op jit(solution)/shard_map/all_gather | solution.py:28
  69.3 4.2 fusion.16
  73.5 7.8 %broadcast_in_dim.13 = f32[128,128,256]{2,1,0:T(8,128)} broadcast(f32[]{:T(128)} %constant.62.clone.1), dimensions={} | broadcast | bytes 16777220 | tf_op jit(solution)/shard_map/broadcast_in_dim | solution.py:44
  81.3 3.7 scatter_fusion
  85.1 0.0 all-to-all-done.1
  85.1 12.4 %all-to-all-start = ((f32[128,128,256]{2,1,0:T(8,128)}), f32[128,128,256]{2,1,0:T(8,128)}, u32[]{:S(2)}, u32[]{:S(2)}) async-start(f32[128,128,256]{2,1,0:T(8,128)} %scatter_fusion), calls=%async_computation | async-start | bytes 33554432 | tf_op jit(solution)/shard_map/all_to_all | solution.py:47
  97.5 0.2 all-gather.9.cloned.1.call-start
  97.8 0.1 compare_convert_fusion
  97.9 0.0 copy-done.4
  97.9 0.1 broadcast_multiply_fusion
  98.0 0.1 copy.31
  98.1 365.0 %all-to-all-done = f32[128,128,256]{2,1,0:T(8,128)} async-done(((f32[128,128,256]{2,1,0:T(8,128)}), f32[128,128,256]{2,1,0:T(8,128)}, u32[]{:S(2)}, u32[]{:S(2)}) %all-to-all-start) | async-done | bytes 16777248 | tf_op jit(solution)/shard_map/all_to_all | solution.py:47
  463.0 17.4 %copy.26 = f32[128,128,256]{1,2,0:T(8,128)} copy(f32[128,128,256]{2,1,0:T(8,128)} %all-to-all-done) | data formatting | bytes 33554432 | tf_op jit(solution)/shard_map/all_to_all | solution.py:47
  480.4 16.5 %copy.32 = f32[64,2,128,2,128]{4,0,3,2,1:T(8,128)} copy(f32[64,2,128,2,128]{2,4,3,1,0:T(8,128)} %bitcast.45) | data formatting | bytes 33554432 | tf_op jit(solution)/shard_map/reshape | solution.py:52
  497.0 9.5 %bitcast_add_fusion = f32[2,128,32,128]{3,2,1,0:T(8,128)S(1)} fusion(f32[64,2,128,2,128]{4,0,3,2,1:T(8,128)} %copy.32, f32[2,128,128]{2,1,0:T(8,128)S(1)} %broadcast_multiply_fusion, f32[2,32]{1,0:T(2,128)S(1)} %compare_convert_fusion, s32[64,2,2]{0,2,1:T(2,128)S(1)} %copy.31), kind=kOutput, calls=%fused_computation.4 | convolution fusion | flops 1612718080 | bytes 21103872 | tf_op jit(solution)/shard_map/srkc,srxky->rxcy/dot_general | solution.py:53
  506.5 3.9 copy.45
  510.4 0.0 copy-start.3
  510.4 2.0 copy-done.3
  512.4 0.6 slice_select_fusion.1
  513.1 0.0 all-gather.9.cloned.1.call-update
  513.1 0.3 all-gather.7.cloned.1.call-start
  513.4 75.6 %all-gather.9.cloned.1.call-done = f32[8192,128]{1,0:T(8,128)} async-done(((f32[128,128]{1,0:T(8,128)}), f32[8192,128]{1,0:T(8,128)}) %all-gather.9.cloned.1.call-update) | async-done | bytes 4194320 | tf_op jit(solution)/shard_map/all_gather | solution.py:9
  589.0 2.4 reduce_sum.18
  591.4 0.1 copy.33
  591.5 11.7 %cholesky.19 = f32[128,128]{1,0:T(8,128)S(1)} custom-call(f32[128,128]{1,0:T(8,128)S(1)} %fusion.5), custom_call_target="Cholesky" | custom-call | tf_op jit(solution)/shard_map/jit(cholesky)/cholesky | solution.py:64
  603.3 0.6 compare_reduce_fusion
  603.9 0.7 select_bitcast_fusion
  604.6 9.8 %custom-call.7 = f32[1,128,128]{1,2,0:T(8,128)S(1)} custom-call(f32[1,128,128]{2,1,0:T(8,128)S(1)} %select_bitcast_fusion), custom_call_target="InvertDiagBlocksLowerTriangular" | custom-call | tf_op jit(solution)/shard_map/jit(_solve_triangular)/triangular_solve | solution.py:65
  614.4 1.2 fusion.1
  615.6 0.7 fusion.3
  616.3 11.3 %all_gather.19 = f32[4,256,128]{2,1,0:T(8,128)S(1)} all-gather(f32[1,256,128]{2,1,0:T(8,128)S(1)} %maximum_select_fusion), channel_id=1, replica_groups=mesh['scen'=64,'link'=4] {'link'}, dimensions={0}, use_global_device_ids=true | all-gather | bytes 655360 | tf_op jit(solution)/shard_map/all_gather | solution.py:9
  627.5 0.7 reduce_sum.19
  628.2 0.0 all-gather.7.cloned.1.call-update
  628.2 0.0 copy-start.1
  628.3 82.2 %all-gather.7.cloned.1.call-done = f32[16384,128]{1,0:T(8,128)} async-done(((f32[256,128]{1,0:T(8,128)}), f32[16384,128]{1,0:T(8,128)}) %all-gather.7.cloned.1.call-update) | async-done | bytes 8388624 | tf_op jit(solution)/shard_map/all_gather | solution.py:68
  710.5 10.4 %convolution_subtract_fusion = f32[256,4096]{1,0:T(8,128)} fusion(f32[256,128]{1,0:T(8,128)} %reduce_sum.19, f32[16384,128]{1,0:T(8,128)} %all-gather.7.cloned.1.call-done, s32[]{:T(128)S(6)} %select_n.58, f32[32,8,32,128]{3,2,1,0:T(8,128)} %bitcast.47), kind=kOutput, calls=%fused_computation.2 | convolution fusion | flops 1611661312 | bytes 10616836 | tf_op jit(solution)/shard_map/dot_general | solution.py:72
  (11 shorter events, 0.1 us)
Async XLA Ops:
  7.2 1.2 copy-start
  7.2 5.7 copy-start.5
  7.2 62.1 %all-gather.5.cloned.1.call-start = ((), (), s32[]{:S(2)}) async-start(), calls=%async_computation.2 | async-start | bytes 5242880 | tf_op jit(solution)/shard_map/all_gather | solution.py:28
  14.8 70.3 %all-to-all-start.1 = ((s32[64,2,2]{1,2,0:T(2,128)}), s32[64,2,2]{1,2,0:T(2,128)S(1)}, u32[]{:S(2)}, u32[]{:S(2)}) async-start(s32[64,2,2]{1,2,0:T(2,128)} %copy.30), calls=%async_computation.1 | async-start | bytes 131072 | tf_op jit(solution)/shard_map/all_to_all | solution.py:48
  85.1 12.8 %copy-start.4 = (f32[2,128]{1,0:T(2,128)S(1)}, f32[2,128]{1,0:T(2,128)}, u32[]{:S(2)}) copy-start(f32[2,128]{1,0:T(2,128)} %param.6) | copy-start | bytes 3076
  85.1 377.9 %all-to-all-start = ((f32[128,128,256]{2,1,0:T(8,128)}), f32[128,128,256]{2,1,0:T(8,128)}, u32[]{:S(2)}, u32[]{:S(2)}) async-start(f32[128,128,256]{2,1,0:T(8,128)} %scatter_fusion), calls=%async_computation | async-start | bytes 33554432 | tf_op jit(solution)/shard_map/all_to_all | solution.py:47
  97.5 491.5 %all-gather.9.cloned.1.call-start = ((), (), s32[]{:S(2)}) async-start(), calls=%async_computation.4 | async-start | bytes 4259840 | tf_op jit(solution)/shard_map/all_gather | solution.py:9
  506.5 3.9 copy-start.2
  510.4 2.0 copy-start.3
  513.1 197.4 %all-gather.7.cloned.1.call-start = ((), (), s32[]{:S(2)}) async-start(), calls=%async_computation.3 | async-start | bytes 8519680 | tf_op jit(solution)/shard_map/all_gather | solution.py:68
  628.2 92.6 %copy-start.1 = (bf16[2,1024,256]{2,1,0:T(8,128)(2,1)S(1)}, bf16[2,1024,256]{2,1,0:T(8,128)(2,1)}, u32[]{:S(2)}) copy-start(bf16[2,1024,256]{2,1,0:T(8,128)(2,1)} %param.5) | copy-start | bytes 3145732
Sparse Core Ops, SparseCore 0:
  12.9 56.2 all-gather.4
  513.2 75.7 all-gather.8
  628.4 82.0 all-gather.6
